TPU v7x, 128 devices: a whole 4x4x4 slice. The times are simulated.
128 devices in a mesh: frame: 16 (over y, x), head: 8 (over z, core).
Axes of the slice: x: 4, y: 4, z: 4, core: 2. Of those that a mesh axis runs over, the one named last changes fastest.
Arguments:
- tokens: bfloat16 [12288, 5120], P('frame', 'head'), may hold values from -40 to 40
- mask_block_frame: int32 [96], replicated, may hold values from 0 to 7, as said below
- attended_key_blocks: int32 [96, 10], replicated, may hold values from 0 to 95, as said below
- frozen_query_key_value: bfloat16 [5120, 3, 3072], P(None, None, 'head'), may hold values from -0.104815686 to 0.104815686
- query_key_value_down_weight: bfloat16 [5120, 192], replicated, may hold values from -0.078125 to 0.078125
- query_key_value_up_weight: bfloat16 [64, 3, 3072], P(None, None, 'head'), may hold values from -0.375 to 0.375
- frozen_output_weight: bfloat16 [3072, 5120], P('head'), may hold values from -0.109375 to 0.109375
- output_down_weight: bfloat16 [3072, 64], P('head'), may hold values from -0.109375 to 0.109375
- output_up_weight: bfloat16 [64, 5120], P(None, 'head'), may hold values from -0.75 to 0.75
Outputs:
- attended_out: bfloat16 [12288, 5120], P('frame', 'head')
Inputs may be any that keep to these rules, and one draw needn't show every extreme that they name: `mask_block_frame`: Non-decreasing along the blocks; every frame from 0 to 7 holds at least one block. `attended_key_blocks`: row b lists 10 distinct key blocks and always includes b itself. Take aligned groups of 6 blocks; for a group of query blocks and another group g groups away (g >= 1), the rows of the first group together name exactly 4 // 2 ** (g - 1) distinct blocks of the second, except that a group exactly 8 groups away is named by exactly the larger of that number and 2.
All inputs are finite; a program needn't handle non-finite values.
Results may differ from a plain program's by a relative error of at most 0.017.
Values may be sent and summed in bfloat16 or wider, within the bound.
A program may use at most 128 MiB of HBM per device.

v0:
```python
import math
import jax
import jax.numpy as jnp
from jax import lax
from jax.sharding import PartitionSpec as P

MODEL_WIDTH = 5120
HEAD_SIZE = 128
BLOCK = 128


def rotate_pairs(values, frame_pos, place):
    time_pairs = (HEAD_SIZE - 4 * (HEAD_SIZE // 6)) // 2
    space_pairs = (HEAD_SIZE - 2 * time_pairs) // 2
    time_freq = 10000.0 ** (-jnp.arange(time_pairs).astype(jnp.float32) / time_pairs)
    space_freq = 10000.0 ** (-jnp.arange(space_pairs).astype(jnp.float32) / space_pairs)
    time_angle = frame_pos[:, None] * time_freq[None, :]
    space_angle = place[:, None] * space_freq[None, :]
    cos_time = jnp.cos(time_angle)[:, None, :]
    sin_time = jnp.sin(time_angle)[:, None, :]
    cos_space = jnp.cos(space_angle)[:, None, :]
    sin_space = jnp.sin(space_angle)[:, None, :]
    first_part = values[:, :, :time_pairs]
    second_part = values[:, :, time_pairs : 2 * time_pairs]
    third_part = values[:, :, 2 * time_pairs : 2 * time_pairs + space_pairs]
    fourth_part = values[:, :, 2 * time_pairs + space_pairs :]
    return jnp.concatenate(
        [
            first_part * cos_time - second_part * sin_time,
            first_part * sin_time + second_part * cos_time,
            third_part * cos_space - fourth_part * sin_space,
            third_part * sin_space + fourth_part * cos_space,
        ],
        axis=-1,
    )


def token_positions(mask_block_frame, block_ids):
    count_blocks = mask_block_frame.shape[0]
    all_blocks = jnp.arange(count_blocks)
    same_frame = mask_block_frame[:, None] == mask_block_frame[None, :]
    first_block = jnp.min(jnp.where(same_frame, all_blocks[None, :], count_blocks), axis=1)
    inner_ids = jnp.arange(BLOCK)
    token_ids = block_ids[:, None] * BLOCK + inner_ids[None, :]
    frame_pos = (
        jnp.broadcast_to(mask_block_frame[block_ids][:, None], token_ids.shape)
        .reshape(-1)
        .astype(jnp.float32)
    )
    place = (token_ids - first_block[block_ids][:, None] * BLOCK).reshape(-1).astype(jnp.float32)
    return (frame_pos, place)


def body(
    tokens,
    mask_block_frame,
    attended_key_blocks,
    frozen_query_key_value,
    query_key_value_down_weight,
    query_key_value_up_weight,
    frozen_output_weight,
    output_down_weight,
    output_up_weight,
):
    tok_rows = tokens.shape[0]
    blocks_here = tok_rows // BLOCK
    local_width = frozen_output_weight.shape[0]
    heads_here = local_width // HEAD_SIZE
    adapter_rank_width = output_up_weight.shape[0]
    listed = attended_key_blocks.shape[1]
    weights_flat = frozen_query_key_value.reshape(MODEL_WIDTH, 3 * local_width)
    rank_segment = lax.all_gather(tokens, "head", axis=1, tiled=True)
    projected_rows = jnp.dot(rank_segment, weights_flat, preferred_element_type=jnp.float32)
    adapter_output_sum = jnp.dot(
        rank_segment, query_key_value_down_weight, preferred_element_type=jnp.float32
    )
    adapter_query_key_value = adapter_output_sum.astype(jnp.bfloat16).reshape(
        tok_rows, 3, adapter_rank_width
    )
    projected_rows = projected_rows.reshape(tok_rows, 3, local_width) + jnp.einsum(
        "ngc,cgz->ngz",
        adapter_query_key_value,
        query_key_value_up_weight,
        preferred_element_type=jnp.float32,
    )
    frame_index = lax.axis_index("frame")
    block_ids = frame_index * blocks_here + jnp.arange(blocks_here, dtype=jnp.int32)
    frame_pos, place = token_positions(mask_block_frame, block_ids)
    queries = rotate_pairs(
        projected_rows[:, 0].reshape(tok_rows, heads_here, HEAD_SIZE), frame_pos, place
    ).astype(jnp.bfloat16)
    keys = rotate_pairs(
        projected_rows[:, 1].reshape(tok_rows, heads_here, HEAD_SIZE), frame_pos, place
    ).astype(jnp.bfloat16)
    key_tiles = keys.reshape(blocks_here, BLOCK, local_width)
    value_tiles = projected_rows[:, 2].astype(jnp.bfloat16).reshape(blocks_here, BLOCK, local_width)
    my_lists = lax.dynamic_slice_in_dim(
        attended_key_blocks, frame_index * blocks_here, blocks_here, 0
    )
    pool_keys, pool_values = (
        lax.all_gather(key_tiles, "frame", axis=0, tiled=True),
        lax.all_gather(value_tiles, "frame", axis=0, tiled=True),
    )
    chosen_keys = pool_keys[my_lists].reshape(blocks_here, listed * BLOCK, heads_here, HEAD_SIZE)
    chosen_values = pool_values[my_lists].reshape(
        blocks_here, listed * BLOCK, heads_here, HEAD_SIZE
    )
    query_tiles = queries.reshape(blocks_here, BLOCK, heads_here, HEAD_SIZE)
    scores = jnp.einsum(
        "nqhd,nkhd->nhqk", query_tiles, chosen_keys, preferred_element_type=jnp.float32
    ) / math.sqrt(HEAD_SIZE)
    row_max = jnp.max(scores, axis=-1, keepdims=True)
    powers = jnp.exp(scores - row_max)
    probs = (powers / jnp.sum(powers, axis=-1, keepdims=True)).astype(jnp.bfloat16)
    attention_result = jnp.einsum(
        "nhqk,nkhd->nqhd", probs, chosen_values, preferred_element_type=jnp.float32
    ).astype(jnp.bfloat16)
    attention_result = attention_result.reshape(tok_rows, local_width)
    adapter_output = lax.psum(
        jnp.dot(attention_result, output_down_weight, preferred_element_type=jnp.float32).astype(
            jnp.bfloat16
        ),
        "head",
    )
    partial_value = jnp.dot(
        attention_result, frozen_output_weight, preferred_element_type=jnp.float32
    )
    frozen_output = lax.psum_scatter(
        partial_value.astype(jnp.bfloat16), "head", scatter_dimension=1, tiled=True
    ).astype(jnp.float32)
    return (
        frozen_output
        + jnp.dot(adapter_output, output_up_weight, preferred_element_type=jnp.float32)
    ).astype(jnp.bfloat16)


def solution(mesh):
    return jax.shard_map(
        body,
        mesh=mesh,
        in_specs=(
            P("frame", "head"),
            P(),
            P(),
            P(None, None, "head"),
            P(),
            P(None, None, "head"),
            P("head", None),
            P("head", None),
            P(None, "head"),
        ),
        out_specs=P("frame", "head"),
        check_vma=False,
    )
```

profile of v0, /device:TPU:0, one launch (start us, length us, event | category | flops | bytes accessed | tf_op | source)
XLA Modules:
  0.0 407.3 jit_solution(18228735309528296065)
XLA Ops:
  6.5 0.7 all-gather.4.cloned.1.call-update
  7.3 1.3 gather_fusion.1
  8.6 0.9 select_reduce_fusion
  9.6 0.6 gather_fusion.2
  10.2 16.2 %copy.37 = bf16[5120,3,384]{0,2,1:T(8,128)(2,1)} copy(bf16[5120,3,384]{2,0,1:T(8,128)(2,1)} %param.12) | data formatting | bytes 23592960 | tf_op args[3]
  26.9 0.6 multiply_cosine_fusion
  27.5 31.6 %all-gather.4.cloned.1.call-done = bf16[768,5120]{1,0:T(8,128)(2,1)} async-done(((bf16[768,640]{1,0:T(8,128)(2,1)}), bf16[768,5120]{1,0:T(8,128)(2,1)}) %all-gather.4.cloned.1.call-update) | async-done | bytes 7864336 | tf_op jit(solution)/shard_map/all_gather | solution.py:72
  59.2 6.1 %convolution_convert_fusion.1 = bf16[768,192]{0,1:T(8,128)(2,1)S(1)} fusion(bf16[768,5120]{1,0:T(8,128)(2,1)} %all-gather.4.cloned.1.call-done, bf16[5120,192]{0,1:T(8,128)(2,1)S(1)} %copy-done), kind=kOutput, calls=%fused_computation.22 | convolution fusion | flops 1510096896 | bytes 10125312 | tf_op jit(solution)/shard_map/dot_general | solution.py:74
  65.3 0.7 fusion.38
  66.0 13.3 %bitcast_add_fusion = f32[768,3,384]{0,2,1:T(8,128)S(1)} fusion(f32[3,768,384]{1,2,0:T(8,128)S(1)} %fusion.38, bf16[5120,3,384]{0,2,1:T(8,128)(2,1)S(1)} %copy-done.2, bf16[768,5120]{1,0:T(8,128)(2,1)} %all-gather.4.cloned.1.call-done), kind=kOutput, calls=%fused_computation.18 | convolution fusion | flops 9060581376 | bytes 26738688 | tf_op jit(solution)/shard_map/dot_general | solution.py:73
  80.0 1.1 copy-done.3
  81.2 0.7 convert_element_type.81
  81.9 1.3 copy.45
  83.2 1.3 slice.81
  84.5 1.1 copy.38
  88.5 70.3 %all-gather.8.cloned.1.call-done = bf16[96,128,384]{2,1,0:T(8,128)(2,1)} async-done(((bf16[6,128,384]{2,1,0:T(8,128)(2,1)}), bf16[96,128,384]{2,1,0:T(8,128)(2,1)}) %all-gather.8.cloned.1.call-update) | async-done | bytes 9437200 | tf_op jit(solution)/shard_map/all_gather | solution.py:101
  158.8 7.7 %gather_fusion.3 = bf16[60,128,384]{2,1,0:T(8,128)(2,1)} fusion(bf16[96,128,384]{2,1,0:T(8,128)(2,1)} %all-gather.8.cloned.1.call-done, s32[1024]{0:T(1024)S(1)} %pad_clamp_fusion.1), kind=kCustom, calls=%fused_computation.3 | custom fusion | bytes 11796720 | tf_op jit(solution)/shard_map/gather | solution.py:104
  166.5 15.9 %reshape.243 = bf16[6,1280,3,128]{3,2,1,0:T(4,128)(2,1)} reshape(bf16[60,128,384]{2,1,0:T(8,128)(2,1)} %gather_fusion.3) | data formatting | bytes 11796480 | tf_op jit(solution)/shard_map/reshape | solution.py:104
  182.4 9.4 %fusion.7 = f32[6,3,128,1280]{3,2,1,0:T(8,128)} fusion(bf16[6,1280,3,128]{3,2,1,0:T(4,128)(2,1)} %reshape.243, bf16[6,128,3,42]{3,1,2,0:T(8,128)(2,1)S(1)} %copy.44, bf16[6,128,3,42]{3,1,2,0:T(8,128)(2,1)S(1)} %copy.43, bf16[6,128,3,22]{3,1,2,0:T(8,128)(2,1)S(1)} %copy.42, bf16[6,128,3,22]{3,1,2,0:T(8,128)(2,1)S(1)} %copy.41), kind=kOutput, calls=%fused_computation.13 | convolution fusion | flops 757334016 | bytes 18284544 | tf_op jit(solution)/shard_map/nqhd,nkhd->nhqk/dot_general | solution.py:109
  191.8 15.6 %fusion.37 = (f32[6,3,128]{2,1,0:T(4,128)S(1)}, f32[6,3,128,1280]{3,2,1,0:T(8,128)}) fusion(f32[6,3,128,1280]{3,2,1,0:T(8,128)} %fusion.7), kind=kOutput, calls=%fused_computation.64 | output fusion | flops 11797759 | bytes 23602176 | tf_op jit(solution)/shard_map/sub | solution.py:113
  207.4 28.7 %all-gather.6.cloned.1.call-done = bf16[96,128,384]{2,1,0:T(8,128)(2,1)} async-done(((bf16[6,128,384]{2,1,0:T(8,128)(2,1)}), bf16[96,128,384]{2,1,0:T(8,128)(2,1)}) %all-gather.6.cloned.1.call-update) | async-done | bytes 9437200 | tf_op jit(solution)/shard_map/all_gather | solution.py:102
  236.1 7.8 %gather_fusion = bf16[60,128,384]{2,1,0:T(8,128)(2,1)} fusion(bf16[96,128,384]{2,1,0:T(8,128)(2,1)} %all-gather.6.cloned.1.call-done, s32[1024]{0:T(1024)S(1)} %pad_clamp_fusion.1), kind=kCustom, calls=%fused_computation | custom fusion | bytes 11796720 | tf_op jit(solution)/shard_map/gather | solution.py:105
  243.9 15.8 %reshape.242 = bf16[6,1280,3,128]{3,2,1,0:T(4,128)(2,1)} reshape(bf16[60,128,384]{2,1,0:T(8,128)(2,1)} %gather_fusion) | data formatting | bytes 11796480 | tf_op jit(solution)/shard_map/reshape | solution.py:105
  259.7 9.2 %fusion.19 = bf16[6,128,3,128]{1,3,2,0:T(8,128)(2,1)S(1)} fusion(f32[6,3,128,1280]{3,2,1,0:T(8,128)} %get-tuple-element.24, f32[6,3,128]{2,1,0:T(4,128)S(1)} %get-tuple-element.23, bf16[6,1280,3,128]{3,2,1,0:T(4,128)(2,1)} %reshape.242), kind=kOutput, calls=%fused_computation.21 | convolution fusion | flops 761167872 | bytes 18293760 | tf_op jit(solution)/shard_map/nhqk,nkhd->nqhd/dot_general | solution.py:115
  269.3 8.8 %convolution_convert_fusion = bf16[768,5120]{1,0:T(8,128)(2,1)} fusion(bf16[384,5120]{1,0:T(8,128)(2,1)} %param.15, bf16[48,8,6,128]{3,2,1,0:T(8,128)(2,1)S(1)} %bitcast.62), kind=kOutput, calls=%fused_computation.11 | convolution fusion | flops 3023831040 | bytes 12386304 | tf_op jit(solution)/shard_map/dot_general | solution.py:125
  278.1 10.6 %copy.54 = bf16[768,5120]{0,1:T(8,128)(2,1)} copy(bf16[768,5120]{1,0:T(8,128)(2,1)} %convolution_convert_fusion) | data formatting | bytes 15728640
  288.9 0.7 copy-done.6
  289.6 0.9 convolution_convert_fusion.2
  290.5 48.4 %reduce-scatter.4.cloned.1.call-done = bf16[640,768]{1,0:T(8,128)(2,1)} async-done(((bf16[5120,768]{1,0:T(8,128)(2,1)}), bf16[640,768]{1,0:T(8,128)(2,1)}) %reduce-scatter.4.cloned.1.call-update) | async-done | bytes 983056
  338.9 1.5 copy.55
  340.4 58.1 %all-reduce.2.cloned.1.call-done = bf16[768,64]{0,1:T(8,128)(2,1)} async-done(((bf16[768,64]{0,1:T(8,128)(2,1)}), bf16[768,64]{0,1:T(8,128)(2,1)}) %all-reduce.2.cloned.1.call-update) | async-done | bytes 98320 | tf_op jit(solution)/shard_map/psum | solution.py:119
  398.5 2.3 add_convert_fusion
  (49 shorter events, 4.8 us)
Async XLA Ops:
  6.5 52.6 %copy-start = (bf16[5120,192]{0,1:T(8,128)(2,1)S(1)}, bf16[5120,192]{0,1:T(8,128)(2,1)}, u32[]{:S(2)}) copy-start(bf16[5120,192]{0,1:T(8,128)(2,1)} %param.13) | copy-start | bytes 5898244
  6.5 52.6 %all-gather.4.cloned.1.call-start = ((), (), s32[]{:S(2)}) async-start(), calls=%async_computation.1 | async-start | bytes 8847360 | tf_op jit(solution)/shard_map/all_gather | solution.py:72
  7.3 151.5 %all-gather.8.cloned.1.call-start = ((), (), s32[]{:S(2)}) async-start(), calls=%async_computation.3 | async-start | bytes 10027008 | tf_op jit(solution)/shard_map/all_gather | solution.py:101
  27.5 37.8 %copy-start.4 = (bf16[64,3,384]{2,0,1:T(8,128)(2,1)S(1)}, bf16[64,3,384]{2,0,1:T(8,128)(2,1)}, u32[]{:S(2)}) copy-start(bf16[64,3,384]{2,0,1:T(8,128)(2,1)} %param.14) | copy-start | bytes 442372
  59.2 6.8 %copy-start.2 = (bf16[5120,3,384]{0,2,1:T(8,128)(2,1)S(1)}, bf16[5120,3,384]{0,2,1:T(8,128)(2,1)}, u32[]{:S(2)}) copy-start(bf16[5120,3,384]{0,2,1:T(8,128)(2,1)} %copy.37) | copy-start | bytes 35389444
  79.3 1.7 copy-start.3
  79.5 6.4 %copy-start.7 = (s32[96,10]{0,1:T(8,128)S(1)}, s32[96,10]{0,1:T(8,128)}, u32[]{:S(2)}) copy-start(s32[96,10]{0,1:T(8,128)} %param.11) | copy-start | bytes 11524
  83.1 152.9 %all-gather.6.cloned.1.call-start = ((), (), s32[]{:S(2)}) async-start(), calls=%async_computation.2 | async-start | bytes 10027008 | tf_op jit(solution)/shard_map/all_gather | solution.py:102
  85.6 253.2 %reduce-scatter.4.cloned.1.call-start = ((), (), s32[]{:S(2)}) async-start(), calls=%async_computation.5 | async-start | bytes 8847360
  288.8 0.8 copy-start.6
  288.8 109.7 %copy-start.5 = (bf16[64,640]{1,0:T(8,128)(2,1)S(1)}, bf16[64,640]{1,0:T(8,128)(2,1)}, u32[]{:S(2)}) copy-start(bf16[64,640]{1,0:T(8,128)(2,1)} %param.17) | copy-start | bytes 245764
  288.8 112.0 %copy-start.1 = (bf16[5120,192]{0,1:T(8,128)(2,1)S(1)}, bf16[5120,192]{0,1:T(8,128)(2,1)}, u32[]{:S(2)}) copy-start(bf16[5120,192]{0,1:T(8,128)(2,1)} %param.13) | copy-start | bytes 5898244
  288.8 109.7 %all-reduce.2.cloned.1.call-start = ((), (), s32[]{:S(2)}) async-start(), calls=%async_computation.4 | async-start | bytes 196608 | tf_op jit(solution)/shard_map/psum | solution.py:119
Sparse Core Ops, SparseCore 0:
  9.0 50.0 all-gather.3
  83.3 75.4 all-gather.7
  160.9 75.1 all-gather.5
  288.9 49.8 reduce-scatter.3
  341.0 57.4 all-reduce.1
where the time goes:
time: 409 us; the launch traced here: 407 us
  waiting for transfers between devices  238 us (58%)
  local copies, waits for them, and re-layouts  86.9 us (21%)
  matrix products  50.6 us (12%)
  other arithmetic  18.3 us (4%)
  between operations  13.3 us (3%)
    all_gather x1, waiting for transfers between devices, body(): lax.all_gather(key_tiles, 'frame', axis=0, tiled=True)  70.3 us
    psum x1, waiting for transfers between devices, body(): lax.psum(jnp.dot(attention_result, output_down_weight, preferred_element_...  58.1 us
    unnamed x6, waiting for transfers between devices  49.2 us
    all_gather x1, waiting for transfers between devices, body(): rank_segment = lax.all_gather(tokens, 'head', axis=1, tiled=True)  31.6 us
    unnamed x19, local copies, waits for them, and re-layouts  30.2 us
    all_gather x1, waiting for transfers between devices, body(): lax.all_gather(value_tiles, 'frame', axis=0, tiled=True)  28.7 us
    reshape x1, local copies, waits for them, and re-layouts, body(): pool_keys[my_lists]  15.9 us
    reshape x1, local copies, waits for them, and re-layouts, body(): pool_values[my_lists]  15.8 us
  transfers between devices with their start and end apart: 5, of which 5 were waited for; matrix products, arithmetic and copies ran while one was open for 19% of the time, Pallas kernels for 0%

commit v1 on v0

--- a/solution.py
+++ b/solution.py
@@ -69,7 +69,9 @@
     adapter_rank_width = output_up_weight.shape[0]
     listed = attended_key_blocks.shape[1]
     weights_flat = frozen_query_key_value.reshape(MODEL_WIDTH, 3 * local_width)
-    rank_segment = lax.all_gather(tokens, "head", axis=1, tiled=True)
+    rank_segment = jnp.concatenate(
+        lax.all_to_all(jnp.stack([tokens] * lax.axis_size("head")), "head", 0, 0), axis=1
+    )
     projected_rows = jnp.dot(rank_segment, weights_flat, preferred_element_type=jnp.float32)
     adapter_output_sum = jnp.dot(
         rank_segment, query_key_value_down_weight, preferred_element_type=jnp.float32

time: 409 us -> 493 us (1.21); the launches traced: 407 us -> 485 us
  local copies, waits for them, and re-layouts: 86.9 us -> 123 us
  waiting for transfers between devices: 238 us -> 266 us
  starting transfers between devices: 0.35 us -> 15.2 us
    all_to_all x0 -> x1, waiting for transfers between devices: none -> 70.4 us  [body(): lax.all_to_all(jnp.stack([tokens] * lax.axis_size('head')), 'head', 0, 0)]
    all_gather x1 -> x0, waiting for transfers between devices: 31.6 us -> none  [body(): rank_segment = lax.all_gather(tokens, 'head', axis=1, tiled=True)]
    reshape x0 -> x3, local copies, waits for them, and re-layouts: none -> 31.3 us  [body(): jnp.concatenate(lax.all_to_all(jnp.stack([tokens] * lax.axis_size('head')...]
    all_gather x1, waiting for transfers between devices: 70.3 us -> 60.4 us  [body(): lax.all_gather(key_tiles, 'frame', axis=0, tiled=True)]
    all_gather x1, starting transfers between devices: 0.04 us -> 9.49 us  [body(): lax.all_gather(value_tiles, 'frame', axis=0, tiled=True)]
    all_to_all x0 -> x1, starting transfers between devices: none -> 5.56 us  [body(): lax.all_to_all(jnp.stack([tokens] * lax.axis_size('head')), 'head', 0, 0)]
    another operation x0 -> x1, local copies, waits for them, and re-layouts: none -> 5.15 us  [body(): jnp.stack([tokens] * lax.axis_size('head'))]
    unnamed x19 -> x27, local copies, waits for them, and re-layouts: 30.2 us -> 28.3 us
  transfers between devices with their start and end apart: 5 -> 5, of which waited for: 5 -> 5; matrix products, arithmetic and copies ran while one was open for 19% -> 15% of each run, Pallas kernels for 0% -> 0%
where the time goes in v1:
time: 493 us; the launch traced here: 485 us
  waiting for transfers between devices  266 us (54%)
  local copies, waits for them, and re-layouts  123 us (25%)
  matrix products  49.4 us (10%)
  other arithmetic  18.2 us (4%)
  starting transfers between devices  15.2 us (3%)
  between operations  13.6 us (3%)
    all_to_all x1, waiting for transfers between devices, body(): lax.all_to_all(jnp.stack([tokens] * lax.axis_size('head')), 'head', 0, 0)  70.4 us
    all_gather x1, waiting for transfers between devices, body(): lax.all_gather(key_tiles, 'frame', axis=0, tiled=True)  60.4 us
    psum x1, waiting for transfers between devices, body(): lax.psum(jnp.dot(attention_result, output_down_weight, preferred_element_...  58.1 us
    unnamed x5, waiting for transfers between devices  48.5 us
    reshape x3, local copies, waits for them, and re-layouts, body(): jnp.concatenate(lax.all_to_all(jnp.stack([tokens] * lax.axis_size('head')...  31.3 us
    all_gather x1, waiting for transfers between devices, body(): lax.all_gather(value_tiles, 'frame', axis=0, tiled=True)  28.6 us
    unnamed x27, local copies, waits for them, and re-layouts  28.3 us
    reshape x1, local copies, waits for them, and re-layouts, body(): pool_keys[my_lists]  15.9 us
  transfers between devices with their start and end apart: 5, of which 5 were waited for; matrix products, arithmetic and copies ran while one was open for 15% of the time, Pallas kernels for 0%

profile of v1, /device:TPU:0, one launch (start us, length us, event | category | flops | bytes accessed | tf_op | source)
XLA Modules:
  0.0 485.0 jit_solution(13645291746598569102)
XLA Ops:
  6.5 5.2 %stack.2 = bf16[8,768,640]{2,1,0:T(8,128)(2,1)} broadcast(bf16[768,640]{1,0:T(8,128)(2,1)} %param.9), dimensions={1,2} | broadcast | bytes 8847360 | tf_op jit(solution)/shard_map/stack | solution.py:73
  11.7 5.6 %all-to-all-start = ((bf16[8,768,640]{2,1,0:T(8,128)(2,1)}), bf16[8,768,640]{2,1,0:T(8,128)(2,1)}, u32[]{:S(2)}, u32[]{:S(2)}) async-start(bf16[8,768,640]{2,1,0:T(8,128)(2,1)} %stack.2), calls=%async_computation | async-start | bytes 15728640 | tf_op jit(solution)/shard_map/all_to_all | solution.py:73
  18.8 15.3 %copy.39 = bf16[5120,3,384]{0,2,1:T(8,128)(2,1)} copy(bf16[5120,3,384]{2,0,1:T(8,128)(2,1)} %param.12) | data formatting | bytes 23592960 | tf_op args[3]
  34.3 1.0 multiply_cosine_fusion.1
  35.9 70.4 %all-to-all-done = bf16[8,768,640]{2,1,0:T(8,128)(2,1)} async-done(((bf16[8,768,640]{2,1,0:T(8,128)(2,1)}), bf16[8,768,640]{2,1,0:T(8,128)(2,1)}, u32[]{:S(2)}, u32[]{:S(2)}) %all-to-all-start) | async-done | bytes 7864352 | tf_op jit(solution)/shard_map/all_to_all | solution.py:73
  106.3 10.9 %copy.38 = bf16[768,8,640]{2,1,0:T(8,128)(2,1)} copy(bf16[768,8,640]{2,0,1:T(8,128)(2,1)} %bitcast) | data formatting | bytes 15728640 | tf_op jit(solution)/shard_map/reshape | solution.py:72
  117.2 12.7 %reshape.251 = bf16[768,5120,1]{1,0,2:T(8,128)(2,1)} reshape(bf16[768,8,640]{2,1,0:T(8,128)(2,1)} %copy.38) | data formatting | bytes 15728640 | tf_op jit(solution)/shard_map/reshape | solution.py:72
  129.9 7.8 %copy.58 = bf16[8,96,8,640]{3,2,0,1:T(8,128)(2,1)} copy(bf16[8,96,8,640]{3,2,1,0:T(8,128)(2,1)} %bitcast.17) | data formatting | bytes 15728640 | tf_op jit(solution)/shard_map/reshape | solution.py:72
  137.7 6.1 %convolution_convert_fusion.1 = bf16[768,192]{0,1:T(8,128)(2,1)S(1)} fusion(bf16[768,5120]{1,0:T(8,128)(2,1)} %bitcast.59, bf16[5120,192]{0,1:T(8,128)(2,1)S(1)} %copy-done), kind=kOutput, calls=%fused_computation.21 | convolution fusion | flops 1510096896 | bytes 10125312 | tf_op jit(solution)/shard_map/dot_general | solution.py:76
  143.8 1.6 fusion.35
  145.4 11.2 %bitcast_add_fusion = f32[768,3,384]{0,2,1:T(8,128)} fusion(f32[3,768,384]{1,2,0:T(8,128)S(1)} %fusion.35, bf16[768,5120,1]{1,0,2:T(8,128)(2,1)S(1)} %copy-done.3, bf16[5120,3,384]{0,2,1:T(8,128)(2,1)S(1)} %bitcast.58), kind=kOutput, calls=%fused_computation.17 | convolution fusion | flops 9060581376 | bytes 26738688 | tf_op jit(solution)/shard_map/dot_general | solution.py:75
  156.7 1.8 fusion.33
  159.9 1.3 copy.47
  161.1 9.5 %all-gather.3.cloned.1.call-start = ((), (), s32[]{:S(2)}) async-start(), calls=%async_computation.2 | async-start | bytes 10027008 | tf_op jit(solution)/shard_map/all_gather | solution.py:104
  170.6 1.4 slice.81
  172.0 1.1 copy.40
  175.8 60.4 %all-gather.5.cloned.1.call-done = bf16[96,128,384]{2,1,0:T(8,128)(2,1)} async-done(((bf16[6,128,384]{2,1,0:T(8,128)(2,1)}), bf16[96,128,384]{2,1,0:T(8,128)(2,1)}) %all-gather.5.cloned.1.call-update) | async-done | bytes 9437200 | tf_op jit(solution)/shard_map/all_gather | solution.py:103
  236.2 7.8 %gather_fusion.3 = bf16[60,128,384]{2,1,0:T(8,128)(2,1)} fusion(bf16[96,128,384]{2,1,0:T(8,128)(2,1)} %all-gather.5.cloned.1.call-done, s32[1024]{0:T(1024)S(1)} %pad_clamp_fusion.1), kind=kCustom, calls=%fused_computation.3 | custom fusion | bytes 11796720 | tf_op jit(solution)/shard_map/gather | solution.py:106
  244.0 15.9 %reshape.254 = bf16[6,1280,3,128]{3,2,1,0:T(4,128)(2,1)} reshape(bf16[60,128,384]{2,1,0:T(8,128)(2,1)} %gather_fusion.3) | data formatting | bytes 11796480 | tf_op jit(solution)/shard_map/reshape | solution.py:106
  259.9 9.4 %fusion.6 = f32[6,3,128,1280]{3,2,1,0:T(8,128)} fusion(bf16[6,1280,3,128]{3,2,1,0:T(4,128)(2,1)} %reshape.254, bf16[6,128,3,42]{3,1,2,0:T(8,128)(2,1)S(1)} %copy.46, bf16[6,128,3,42]{3,1,2,0:T(8,128)(2,1)S(1)} %copy.45, bf16[6,128,3,22]{3,1,2,0:T(8,128)(2,1)S(1)} %copy.44, bf16[6,128,3,22]{3,1,2,0:T(8,128)(2,1)S(1)} %copy.43), kind=kOutput, calls=%fused_computation.12 | convolution fusion | flops 757334016 | bytes 18284544 | tf_op jit(solution)/shard_map/nqhd,nkhd->nhqk/dot_general | solution.py:111
  269.3 15.6 %fusion.34 = (f32[6,3,128]{2,1,0:T(4,128)S(1)}, f32[6,3,128,1280]{3,2,1,0:T(8,128)}) fusion(f32[6,3,128,1280]{3,2,1,0:T(8,128)} %fusion.6), kind=kOutput, calls=%fused_computation.63 | output fusion | flops 11797759 | bytes 23602176 | tf_op jit(solution)/shard_map/sub | solution.py:115
  284.9 28.6 %all-gather.3.cloned.1.call-done = bf16[96,128,384]{2,1,0:T(8,128)(2,1)} async-done(((bf16[6,128,384]{2,1,0:T(8,128)(2,1)}), bf16[96,128,384]{2,1,0:T(8,128)(2,1)}) %all-gather.3.cloned.1.call-update) | async-done | bytes 9437200 | tf_op jit(solution)/shard_map/all_gather | solution.py:104
  313.5 7.8 %gather_fusion = bf16[60,128,384]{2,1,0:T(8,128)(2,1)} fusion(bf16[96,128,384]{2,1,0:T(8,128)(2,1)} %all-gather.3.cloned.1.call-done, s32[1024]{0:T(1024)S(1)} %pad_clamp_fusion.1), kind=kCustom, calls=%fused_computation | custom fusion | bytes 11796720 | tf_op jit(solution)/shard_map/gather | solution.py:107
  321.3 15.8 %reshape.253 = bf16[6,1280,3,128]{3,2,1,0:T(4,128)(2,1)} reshape(bf16[60,128,384]{2,1,0:T(8,128)(2,1)} %gather_fusion) | data formatting | bytes 11796480 | tf_op jit(solution)/shard_map/reshape | solution.py:107
  337.2 9.2 %fusion.16 = bf16[6,128,3,128]{1,3,2,0:T(8,128)(2,1)S(1)} fusion(f32[6,3,128,1280]{3,2,1,0:T(8,128)} %get-tuple-element.24, f32[6,3,128]{2,1,0:T(4,128)S(1)} %get-tuple-element.23, bf16[6,1280,3,128]{3,2,1,0:T(4,128)(2,1)} %reshape.253), kind=kOutput, calls=%fused_computation.20 | convolution fusion | flops 761167872 | bytes 18293760 | tf_op jit(solution)/shard_map/nhqk,nkhd->nqhd/dot_general | solution.py:117
  346.8 8.8 %convolution_convert_fusion = bf16[768,5120]{1,0:T(8,128)(2,1)} fusion(bf16[384,5120]{1,0:T(8,128)(2,1)} %param.15, bf16[48,8,6,128]{3,2,1,0:T(8,128)(2,1)S(1)} %bitcast.64), kind=kOutput, calls=%fused_computation.11 | convolution fusion | flops 3023831040 | bytes 12386304 | tf_op jit(solution)/shard_map/dot_general | solution.py:127
  355.5 10.6 %copy.56 = bf16[768,5120]{0,1:T(8,128)(2,1)} copy(bf16[768,5120]{1,0:T(8,128)(2,1)} %convolution_convert_fusion) | data formatting | bytes 15728640
  367.0 0.9 convolution_convert_fusion.2
  367.8 48.4 %reduce-scatter.4.cloned.1.call-done = bf16[640,768]{1,0:T(8,128)(2,1)} async-done(((bf16[5120,768]{1,0:T(8,128)(2,1)}), bf16[640,768]{1,0:T(8,128)(2,1)}) %reduce-scatter.4.cloned.1.call-update) | async-done | bytes 983056
  416.2 1.5 copy.57
  417.8 58.1 %all-reduce.2.cloned.1.call-done = bf16[768,64]{0,1:T(8,128)(2,1)} async-done(((bf16[768,64]{0,1:T(8,128)(2,1)}), bf16[768,64]{0,1:T(8,128)(2,1)}) %all-reduce.2.cloned.1.call-update) | async-done | bytes 98320 | tf_op jit(solution)/shard_map/psum | solution.py:121
  475.9 2.3 add_convert_fusion
  (61 shorter events, 7.5 us)
Async XLA Ops:
  6.5 131.2 %copy-start = (bf16[5120,192]{0,1:T(8,128)(2,1)S(1)}, bf16[5120,192]{0,1:T(8,128)(2,1)}, u32[]{:S(2)}) copy-start(bf16[5120,192]{0,1:T(8,128)(2,1)} %param.13) | copy-start | bytes 5898244
  11.7 5.6 %copy-start.2 = (s32[96]{0:T(128)S(1)}, s32[96]{0:T(128)}, u32[]{:S(2)}) copy-start(s32[96]{0:T(128)} %param.10) | copy-start | bytes 1156
  11.7 94.6 %all-to-all-start = ((bf16[8,768,640]{2,1,0:T(8,128)(2,1)}), bf16[8,768,640]{2,1,0:T(8,128)(2,1)}, u32[]{:S(2)}, u32[]{:S(2)}) async-start(bf16[8,768,640]{2,1,0:T(8,128)(2,1)} %stack.2), calls=%async_computation | async-start | bytes 15728640 | tf_op jit(solution)/shard_map/all_to_all | solution.py:73
  17.3 219.0 %all-gather.5.cloned.1.call-start = ((), (), s32[]{:S(2)}) async-start(), calls=%async_computation.3 | async-start | bytes 10027008 | tf_op jit(solution)/shard_map/all_gather | solution.py:103
  129.9 15.5 %slice-start = ((s8[11796480]{0:T(1024)(128)(4,1)}), s8[3407872]{0:T(1024)(128)(4,1)S(1)}, s32[]{:S(2)}) async-start(s8[11796480]{0:T(1024)(128)(4,1)} %bitcast.57), calls=%async_computation.6 | async-start | bytes 6815744
  129.9 15.5 %slice-start.1 = ((s8[11796480]{0:T(1024)(128)(4,1)}), s8[4194304]{0:T(1024)(128)(4,1)S(1)}, s32[]{:S(2)}) async-start(s8[11796480]{0:T(1024)(128)(4,1)} %bitcast.57), calls=%async_computation.7 | async-start | bytes 8388608
  137.7 7.7 %slice-start.2 = ((s8[11796480]{0:T(1024)(128)(4,1)}), s8[4194304]{0:T(1024)(128)(4,1)S(1)}, s32[]{:S(2)}) async-start(s8[11796480]{0:T(1024)(128)(4,1)} %bitcast.57), calls=%async_computation.8 | async-start | bytes 8388608
  137.7 7.7 %copy-start.3 = (bf16[768,5120,1]{1,0,2:T(8,128)(2,1)S(1)}, bf16[768,5120,1]{1,0,2:T(8,128)(2,1)}, u32[]{:S(2)}) copy-start(bf16[768,5120,1]{1,0,2:T(8,128)(2,1)} %reshape.251) | copy-start | bytes 23592964
  156.7 2.2 copy-start.4
  156.7 2.2 copy-start.5
  158.5 14.7 %copy-start.8 = (s32[96,10]{0,1:T(8,128)S(1)}, s32[96,10]{0,1:T(8,128)}, u32[]{:S(2)}) copy-start(s32[96,10]{0,1:T(8,128)} %param.11) | copy-start | bytes 11524
  161.1 152.4 %all-gather.3.cloned.1.call-start = ((), (), s32[]{:S(2)}) async-start(), calls=%async_computation.2 | async-start | bytes 10027008 | tf_op jit(solution)/shard_map/all_gather | solution.py:104
  173.1 243.1 %reduce-scatter.4.cloned.1.call-start = ((), (), s32[]{:S(2)}) async-start(), calls=%async_computation.5 | async-start | bytes 8847360
  366.2 0.8 copy-start.7
  366.2 109.7 %copy-start.6 = (bf16[64,640]{1,0:T(8,128)(2,1)S(1)}, bf16[64,640]{1,0:T(8,128)(2,1)}, u32[]{:S(2)}) copy-start(bf16[64,640]{1,0:T(8,128)(2,1)} %param.17) | copy-start | bytes 245764
  366.2 112.0 %copy-start.1 = (bf16[5120,192]{0,1:T(8,128)(2,1)S(1)}, bf16[5120,192]{0,1:T(8,128)(2,1)}, u32[]{:S(2)}) copy-start(bf16[5120,192]{0,1:T(8,128)(2,1)} %param.13) | copy-start | bytes 5898244
  366.2 109.7 %all-reduce.2.cloned.1.call-start = ((), (), s32[]{:S(2)}) async-start(), calls=%async_computation.4 | async-start | bytes 196608 | tf_op jit(solution)/shard_map/psum | solution.py:121
Sparse Core Ops, SparseCore 0:
  161.3 74.9 all-gather.4
  238.4 75.1 all-gather.2
  366.3 49.8 reduce-scatter.3
  418.4 57.4 all-reduce.1
